TPU v7x, 32 devices: a whole 2x2x4 slice. The times are simulated.
32 devices in a mesh: row: 4 (over z), col: 4 (over x, core), layer: 2 (over y).
Axes of the slice: x: 2, y: 2, z: 4, core: 2. Of those that a mesh axis runs over, the one named last changes fastest.
Arguments:
- intersection: bfloat16 [2048, 2, 1024], P('row', 'layer', 'col'), may hold values from -6 to 6
- density: bfloat16 [2, 1024, 2, 1024], P('layer', 'row', None, 'col'), may hold values from -0.125 to 0.125
- hamiltonian: bfloat16 [2, 1024, 2, 1024], P('layer', 'row', None, 'col'), may hold values from -0.125 to 0.125
- intersection_pattern: int32 [16, 2, 8], P('row', 'layer', 'col'), may hold values 0 or 1
- density_pattern: int32 [2, 8, 2, 8], P('layer', 'row', None, 'col'), may hold values 0 or 1
- hamiltonian_pattern: int32 [2, 8, 2, 8], P('layer', 'row', None, 'col'), may hold values 0 or 1
- product_filter: int32 [16, 2, 8], P('row', 'layer', 'col'), may hold values 0 or 1
Outputs:
- gradient_term: bfloat16 [2048, 2, 1024], P('row', 'layer', 'col')
All inputs are finite; a program needn't handle non-finite values. No bound on the sum of `intersection_pattern` or of `density_pattern` or of `hamiltonian_pattern` or of `product_filter` on one device may be relied on, other than what follows from the above.
Results may differ from a plain program's by a relative error of at most 0.005.
Values may be sent and summed in bfloat16 or wider, within the bound.
No kernel may reach another device: no remote copies, remote signals or barrier semaphores. Data moves between devices by JAX's collectives and lax.ppermute only.
A program may use at most 64 MiB of HBM per device.

v0:
```python
import jax
import jax.numpy as jnp
from jax import lax
from jax.sharding import PartitionSpec as P


def mask_left(block_tile, pattern):
    row_count, _, col_count = block_tile.shape
    row_blocks = pattern.shape[0]
    col_blocks = pattern.shape[2]
    blocks = block_tile.reshape(
        row_blocks, row_count // row_blocks, col_blocks, col_count // col_blocks
    )
    blocks = blocks * pattern.reshape(row_blocks, 1, col_blocks, 1).astype(jnp.bfloat16)
    return blocks.reshape(row_count, col_count)


def mask_right(block_tile, pattern):
    _, row_count, layers, col_count = block_tile.shape
    row_blocks = pattern.shape[1]
    col_blocks = pattern.shape[3]
    blocks = block_tile.reshape(
        row_blocks, row_count // row_blocks, layers, col_blocks, col_count // col_blocks
    )
    blocks = blocks * pattern.reshape(row_blocks, 1, layers, col_blocks, 1).astype(jnp.bfloat16)
    return blocks.reshape(row_count, layers * col_count)


def multiply(left_tile, right_tile):
    whole_left = lax.all_gather(left_tile, "col", axis=1, tiled=True)
    row_count = whole_left.shape[0]
    layers = lax.axis_size("layer")
    column_span = right_tile.shape[1] // layers
    partial_value = jnp.dot(
        whole_left,
        lax.all_gather(right_tile, "row", axis=0, tiled=True),
        preferred_element_type=jnp.float32,
    )
    return lax.psum_scatter(
        partial_value.reshape(row_count, layers, column_span),
        "layer",
        scatter_dimension=1,
        tiled=True,
    )


def local(
    intersection,
    density,
    hamiltonian,
    intersection_pattern,
    density_pattern,
    hamiltonian_pattern,
    product_filter,
):
    left_factor = mask_left(intersection, intersection_pattern)
    right_factor = mask_right(density, density_pattern)
    raw_product = multiply(left_factor, right_factor)
    filtered = mask_left(raw_product.astype(jnp.bfloat16), product_filter)
    masked_ham = mask_right(hamiltonian, hamiltonian_pattern)
    return multiply(filtered, masked_ham).astype(jnp.bfloat16)


def solution(mesh):
    placed = (
        P("row", "layer", "col"),
        P("layer", "row", None, "col"),
        P("layer", "row", None, "col"),
        P("row", "layer", "col"),
        P("layer", "row", None, "col"),
        P("layer", "row", None, "col"),
        P("row", "layer", "col"),
    )
    return jax.shard_map(
        local, mesh=mesh, in_specs=placed, out_specs=P("row", "layer", "col"), check_vma=False
    )
```

profile of v0, /device:TPU:0, one launch (start us, length us, event | category | flops | bytes accessed | tf_op | source)
XLA Modules:
  0.0 161.6 jit_solution(11556054652740069047)
XLA Ops:
  6.5 0.0 all-gather.7.cloned.1.call-start
  6.5 0.7 convert_bitcast_fusion.1
  7.2 0.2 mul.47
  7.4 0.0 copy-start.1
  7.4 0.1 mul.48
  7.6 0.8 copy-done.1
  8.4 0.0 copy-start.4
  8.4 0.8 mul.49
  9.2 0.0 copy-start
  9.2 0.0 all-gather.7.cloned.1.call-update
  9.2 0.0 all-gather.5.cloned.1.call-start
  9.3 0.0 copy-done.4
  9.3 0.1 copy.8
  9.4 0.2 mul.44
  9.6 0.5 copy-done
  10.2 0.7 bitcast_multiply_fusion.1
  10.9 0.0 all-gather.5.cloned.1.call-update
  10.9 0.0 reduce-scatter.3.cloned.1.call-start
  11.0 29.0 %all-gather.7.cloned.1.call-done = bf16[1024,512]{1,0:T(8,128)(2,1)} async-done(((bf16[256,512]{1,0:T(8,128)(2,1)}), bf16[1024,512]{1,0:T(8,128)(2,1)}) %all-gather.7.cloned.1.call-update) | async-done | bytes 1048592 | tf_op jit(solution)/shard_map/all_gather | solution.py:36
  40.0 17.9 %all-gather.5.cloned.1.call-done = bf16[512,1024]{1,0:T(8,128)(2,1)} async-done(((bf16[512,256]{1,0:T(8,128)(2,1)}), bf16[512,1024]{1,0:T(8,128)(2,1)}) %all-gather.5.cloned.1.call-update) | async-done | bytes 1048592 | tf_op jit(solution)/shard_map/all_gather | solution.py:30
  57.9 3.3 %fusion = f32[512,512]{0,1:T(8,128)} fusion(bf16[512,1024]{1,0:T(8,128)(2,1)} %all-gather.5.cloned.1.call-done, bf16[1024,512]{1,0:T(8,128)(2,1)} %all-gather.7.cloned.1.call-done), kind=kOutput, calls=%fused_computation.6 | convolution fusion | flops 536870912 | bytes 3145728 | tf_op jit(solution)/shard_map/dot_general | solution.py:34
  61.2 0.0 copy-start.3
  61.2 0.0 reduce-scatter.3.cloned.1.call-update
  61.2 0.0 all-gather.11.cloned.1.call-start
  61.3 0.6 copy-done.3
  61.9 0.2 mul.53
  62.1 0.0 copy-start.2
  62.1 0.1 mul.54
  62.2 0.8 copy-done.2
  63.1 0.8 mul.55
  63.9 0.0 copy-start.5
  63.9 0.0 all-gather.11.cloned.1.call-update
  63.9 0.0 all-gather.9.cloned.1.call-start
  64.0 0.6 copy-done.5
  64.6 17.1 %reduce-scatter.3.cloned.1.call-done = f32[512,1,256]{0,2,1:T(8,128)} async-done(((f32[512,2,256]{0,2,1:T(8,128)}), f32[512,1,256]{0,2,1:T(8,128)}) %reduce-scatter.3.cloned.1.call-update) | async-done | bytes 524304 | tf_op jit(solution)/shard_map/reduce_scatter | solution.py:39
  81.7 0.1 mul.50
  81.9 1.8 %bitcast_multiply_fusion = bf16[512,256]{0,1:T(8,128)(2,1)} fusion(bf16[32,8,4,128]{3,2,1,0:T(4,128)(2,1)S(1)} %bitcast.39, f32[512,1,256]{0,2,1:T(8,128)} %reduce-scatter.3.cloned.1.call-done), kind=kLoop, calls=%fused_computation | loop fusion | flops 262144 | bytes 1048576 | tf_op jit(solution)/shard_map/mul | solution.py:14
  83.7 0.0 all-gather.9.cloned.1.call-update
  83.7 0.0 reduce-scatter.5.cloned.1.call-start
  83.7 27.4 %all-gather.11.cloned.1.call-done = bf16[1024,512]{1,0:T(8,128)(2,1)} async-done(((bf16[256,512]{1,0:T(8,128)(2,1)}), bf16[1024,512]{1,0:T(8,128)(2,1)}) %all-gather.11.cloned.1.call-update) | async-done | bytes 1048592 | tf_op jit(solution)/shard_map/all_gather | solution.py:36
  111.2 17.7 %all-gather.9.cloned.1.call-done = bf16[512,1024]{0,1:T(8,128)(2,1)} async-done(((bf16[512,256]{0,1:T(8,128)(2,1)}), bf16[512,1024]{0,1:T(8,128)(2,1)}) %all-gather.9.cloned.1.call-update) | async-done | bytes 1048592 | tf_op jit(solution)/shard_map/all_gather | solution.py:30
  128.9 2.3 %fusion.1 = f32[512,512]{0,1:T(8,128)S(1)} fusion(bf16[512,1024]{0,1:T(8,128)(2,1)} %all-gather.9.cloned.1.call-done, bf16[1024,512]{1,0:T(8,128)(2,1)} %all-gather.11.cloned.1.call-done), kind=kOutput, calls=%fused_computation.7 | convolution fusion | flops 536870912 | bytes 3145728 | tf_op jit(solution)/shard_map/dot_general | solution.py:34
  131.2 1.3 copy.9
  132.5 0.0 reduce-scatter.5.cloned.1.call-update
  132.5 20.5 %reduce-scatter.5.cloned.1.call-done = f32[512,1,256]{2,0,1:T(8,128)} async-done(((f32[512,2,256]{2,0,1:T(8,128)}), f32[512,1,256]{2,0,1:T(8,128)}) %reduce-scatter.5.cloned.1.call-update) | async-done | bytes 524304 | tf_op jit(solution)/shard_map/reduce_scatter | solution.py:39
  153.0 1.8 %convert_element_type.59 = bf16[512,1,256]{2,0,1:T(8,128)(2,1)} convert(f32[512,1,256]{2,0,1:T(8,128)} %reduce-scatter.5.cloned.1.call-done) | non-fusion elementwise | flops 131072 | bytes 786432 | tf_op jit(solution)/shard_map/convert_element_type | solution.py:61
  (5 shorter events, 0.1 us)
Async XLA Ops:
  6.5 33.5 %all-gather.7.cloned.1.call-start = ((), (), s32[]{:S(2)}) async-start(), calls=%async_computation.3 | async-start | bytes 1310720 | tf_op jit(solution)/shard_map/all_gather | solution.py:36
  7.4 1.0 copy-start.1
  8.4 0.9 copy-start.4
  9.2 0.9 copy-start
  9.2 48.7 %all-gather.5.cloned.1.call-start = ((), (), s32[]{:S(2)}) async-start(), calls=%async_computation.2 | async-start | bytes 1310720 | tf_op jit(solution)/shard_map/all_gather | solution.py:30
  10.9 70.8 %reduce-scatter.3.cloned.1.call-start = ((), (), s32[]{:S(2)}) async-start(), calls=%async_computation.4 | async-start | bytes 1572864 | tf_op jit(solution)/shard_map/reduce_scatter | solution.py:39
  61.2 0.7 copy-start.3
  61.2 49.9 %all-gather.11.cloned.1.call-start = ((), (), s32[]{:S(2)}) async-start(), calls=%async_computation.6 | async-start | bytes 1310720 | tf_op jit(solution)/shard_map/all_gather | solution.py:36
  62.1 1.0 copy-start.2
  63.9 0.7 copy-start.5
  63.9 65.0 %all-gather.9.cloned.1.call-start = ((), (), s32[]{:S(2)}) async-start(), calls=%async_computation.5 | async-start | bytes 1310720 | tf_op jit(solution)/shard_map/all_gather | solution.py:30
  83.7 69.3 %reduce-scatter.5.cloned.1.call-start = ((), (), s32[]{:S(2)}) async-start(), calls=%async_computation.7 | async-start | bytes 1572864 | tf_op jit(solution)/shard_map/reduce_scatter | solution.py:39
Sparse Core Ops, SparseCore 0:
  9.4 30.6 all-gather.6
  41.6 16.3 all-gather.4
  61.4 20.3 reduce-scatter.2
  83.2 27.9 all-gather.10
  112.7 16.2 all-gather.8
  132.7 20.3 reduce-scatter.4
where the time goes:
time: 162 us
  waiting for transfers between devices  130 us (80%)
  between operations  13.6 us (8%)
  other arithmetic  6.58 us (4%)
  local copies, waits for them, and re-layouts  5.88 us (4%)
  matrix products  5.57 us (3%)
    all_gather x2, waiting for transfers between devices, multiply(): lax.all_gather(right_tile, 'row', axis=0, tiled=True)  56.5 us
    reduce_scatter x2, waiting for transfers between devices, multiply(): lax.psum_scatter(partial_value.reshape(row_count, layers, column_span), '...  37.6 us
    all_gather x2, waiting for transfers between devices, multiply(): whole_left = lax.all_gather(left_tile, 'col', axis=1, tiled=True)  35.6 us
    dot_general x2, matrix products, multiply(): jnp.dot(whole_left, lax.all_gather(right_tile, 'row', axis=0, tiled=True)...  5.57 us
    unnamed x14, local copies, waits for them, and re-layouts  3.49 us
  transfers between devices with their start and end apart: 6, of which 6 were waited for; matrix products, arithmetic and copies ran while one was open for 3% of the time, Pallas kernels for 0%

commit v1 on v0

--- a/solution.py
+++ b/solution.py
@@ -2,6 +2,27 @@
 import jax.numpy as jnp
 from jax import lax
 from jax.sharding import PartitionSpec as P
+
+
+def collect(array, axis, dim):
+    size, index, rows = (lax.axis_size(axis), lax.axis_index(axis), array.shape[dim])
+    right = [(i, (i + 1) % size) for i in range(size)]
+    left = [(i, (i - 1) % size) for i in range(size)]
+    result = jnp.zeros((*array.shape[:dim], size * rows, *array.shape[dim + 1 :]), array.dtype)
+    result = lax.dynamic_update_slice_in_dim(result, array, index * rows, axis=dim)
+    from_left = from_right = array
+    middle = size // 2
+    for step in range(1, middle + 1):
+        from_left = lax.ppermute(from_left, axis, right)
+        result = lax.dynamic_update_slice_in_dim(
+            result, from_left, (index - step) % size * rows, axis=dim
+        )
+        if step < size - middle:
+            from_right = lax.ppermute(from_right, axis, left)
+            result = lax.dynamic_update_slice_in_dim(
+                result, from_right, (index + step) % size * rows, axis=dim
+            )
+    return result
 
 
 def mask_left(block_tile, pattern):
@@ -32,9 +53,7 @@
     layers = lax.axis_size("layer")
     column_span = right_tile.shape[1] // layers
     partial_value = jnp.dot(
-        whole_left,
-        lax.all_gather(right_tile, "row", axis=0, tiled=True),
-        preferred_element_type=jnp.float32,
+        whole_left, collect(right_tile, "row", 0), preferred_element_type=jnp.float32
     )
     return lax.psum_scatter(
         partial_value.reshape(row_count, layers, column_span),

time: 162 us -> 112 us (0.69)
  waiting for transfers between devices: 130 us -> 72.6 us
  starting transfers between devices: 0.21 us -> 9.18 us
    all_gather x2 -> x0, waiting for transfers between devices: 56.5 us -> none  [multiply(): lax.all_gather(right_tile, 'row', axis=0, tiled=True)]
    all_gather x2, waiting for transfers between devices: 35.6 us -> 0.04 us  [multiply(): whole_left = lax.all_gather(left_tile, 'col', axis=1, tiled=True)]
    ppermute x0 -> x6, waiting for transfers between devices: none -> 34.7 us  [the longest x4 26.1 us: collect(): from_left = lax.ppermute(from_left, axis, right)]
    ppermute x0 -> x6, starting transfers between devices: none -> 9.05 us  [the longest x4 4.62 us: collect(): from_left = lax.ppermute(from_left, axis, right)]
  transfers between devices with their start and end apart: 6 -> 10, of which waited for: 6 -> 8; matrix products, arithmetic and copies ran while one was open for 3% -> 1% of each run, Pallas kernels for 0% -> 0%
where the time goes in v1:
time: 112 us
  waiting for transfers between devices  72.6 us (65%)
  between operations  13.3 us (12%)
  starting transfers between devices  9.18 us (8%)
  local copies, waits for them, and re-layouts  6.39 us (6%)
  other arithmetic  5.22 us (5%)
  matrix products  4.95 us (4%)
    reduce_scatter x2, waiting for transfers between devices, multiply(): lax.psum_scatter(partial_value.reshape(row_count, layers, column_span), '...  37.8 us
    ppermute x4, waiting for transfers between devices, collect(): from_left = lax.ppermute(from_left, axis, right)  26.1 us
    ppermute x2, waiting for transfers between devices, collect(): from_right = lax.ppermute(from_right, axis, left)  8.64 us
    dot_general x2, matrix products, multiply(): jnp.dot(whole_left, collect(right_tile, 'row', 0), preferred_element_type...  4.95 us
    ppermute x4, starting transfers between devices, collect(): from_left = lax.ppermute(from_left, axis, right)  4.62 us
    ppermute x2, starting transfers between devices, collect(): from_right = lax.ppermute(from_right, axis, left)  4.43 us
    unnamed x14, local copies, waits for them, and re-layouts  3.71 us
    mul x2, other arithmetic, mask_left(): blocks * pattern.reshape(row_blocks, 1, col_blocks, 1).astype(jnp.bfloat16)  2.55 us
  transfers between devices with their start and end apart: 10, of which 8 were waited for; matrix products, arithmetic and copies ran while one was open for 1% of the time, Pallas kernels for 0%

profile of v1, /device:TPU:0, one launch (start us, length us, event | category | flops | bytes accessed | tf_op | source)
XLA Modules:
  0.0 111.6 jit_solution(12681633929771606329)
XLA Ops:
  6.5 0.0 all-gather.3.cloned.1.call-start
  6.5 0.7 convert_bitcast_fusion.3
  7.3 0.1 copy.8
  7.4 0.2 mul.60
  7.6 0.0 copy-done
  7.6 0.7 bitcast_multiply_fusion.1
  8.3 0.0 all-gather.3.cloned.1.call-update
  8.4 0.0 reduce-scatter.3.cloned.1.call-start
  8.4 0.9 copy-done.1
  9.3 0.6 copy-done.3
  10.0 0.2 mul.63
  10.2 0.1 mul.64
  10.3 0.1 broadcast.10.clone
  10.4 0.1 constant_dynamic-update-slice_fusion.7
  10.5 3.1 %collective-permute-start = (bf16[256,512]{1,0:T(8,128)(2,1)S(1)}, bf16[256,512]{1,0:T(8,128)(2,1)S(1)}, u32[]{:S(2)}, u32[]{:S(2)}) collective-permute-start(bf16[256,512]{1,0:T(8,128)(2,1)S(1)} %get-tuple-element.8), channel_id=1, source_target_pairs={{0,8},{8,16},{16,24},{24,0},{1,9},{9,17},{17,25},{25,1},{2,10},{10... | collective-permute-start | bytes 786440 | tf_op jit(solution)/shard_map/ppermute | solution.py:16
  13.5 2.1 %collective-permute-start.1 = (bf16[256,512]{1,0:T(8,128)(2,1)S(1)}, bf16[256,512]{1,0:T(8,128)(2,1)S(1)}, u32[]{:S(2)}, u32[]{:S(2)}) collective-permute-start(bf16[256,512]{1,0:T(8,128)(2,1)S(1)} %get-tuple-element.8), channel_id=1, source_target_pairs={{0,24},{8,0},{16,8},{24,16},{1,25},{9,1},{17,9},{25,17},{2,26},{10... | collective-permute-start | bytes 786440 | tf_op jit(solution)/shard_map/ppermute | solution.py:21
  15.6 7.1 %collective-permute-done = bf16[256,512]{1,0:T(8,128)(2,1)S(1)} collective-permute-done((bf16[256,512]{1,0:T(8,128)(2,1)S(1)}, bf16[256,512]{1,0:T(8,128)(2,1)S(1)}, u32[]{:S(2)}, u32[]{:S(2)}) %collective-permute-start) | collective-permute-done | bytes 262176 | tf_op jit(solution)/shard_map/ppermute | solution.py:16
  22.7 0.0 collective-permute-start.2
  22.8 4.4 %collective-permute-done.1 = bf16[256,512]{1,0:T(8,128)(2,1)S(1)} collective-permute-done((bf16[256,512]{1,0:T(8,128)(2,1)S(1)}, bf16[256,512]{1,0:T(8,128)(2,1)S(1)}, u32[]{:S(2)}, u32[]{:S(2)}) %collective-permute-start.1) | collective-permute-done | bytes 262176 | tf_op jit(solution)/shard_map/ppermute | solution.py:21
  27.2 6.0 %collective-permute-done.2 = bf16[256,512]{1,0:T(8,128)(2,1)S(1)} collective-permute-done((bf16[256,512]{1,0:T(8,128)(2,1)S(1)}, bf16[256,512]{1,0:T(8,128)(2,1)S(1)}, u32[]{:S(2)}, u32[]{:S(2)}) %collective-permute-start.2) | collective-permute-done | bytes 262176 | tf_op jit(solution)/shard_map/ppermute | solution.py:16
  33.2 0.0 all-gather.3.cloned.1.call-done
  33.2 3.0 %fusion = f32[512,512]{0,1:T(8,128)} fusion(bf16[512,1024]{1,0:T(8,128)(2,1)} %all-gather.3.cloned.1.call-done, bf16[1024,512]{1,0:T(8,128)(2,1)S(1)} %constant_dynamic-update-slice_fusion.4), kind=kOutput, calls=%fused_computation.14 | convolution fusion | flops 536870912 | bytes 3145728 | tf_op jit(solution)/shard_map/dot_general | solution.py:55
  36.2 0.0 reduce-scatter.3.cloned.1.call-update
  36.2 0.0 all-gather.5.cloned.1.call-start
  36.3 0.6 copy-done.5
  36.9 19.1 %reduce-scatter.3.cloned.1.call-done = f32[512,1,256]{0,2,1:T(8,128)} async-done(((f32[512,2,256]{0,2,1:T(8,128)}), f32[512,1,256]{0,2,1:T(8,128)}) %reduce-scatter.3.cloned.1.call-update) | async-done | bytes 524304 | tf_op jit(solution)/shard_map/reduce_scatter | solution.py:58
  56.0 0.1 mul.70
  56.2 1.8 %bitcast_multiply_fusion = bf16[512,256]{0,1:T(8,128)(2,1)} fusion(bf16[32,8,4,128]{3,2,1,0:T(4,128)(2,1)S(1)} %bitcast.39, f32[512,1,256]{0,2,1:T(8,128)} %reduce-scatter.3.cloned.1.call-done), kind=kLoop, calls=%fused_computation | loop fusion | flops 262144 | bytes 1048576 | tf_op jit(solution)/shard_map/mul | solution.py:35
  58.0 0.0 all-gather.5.cloned.1.call-update
  58.0 0.0 reduce-scatter.5.cloned.1.call-start
  58.0 0.9 copy-done.2
  58.9 0.6 copy-done.4
  59.6 0.2 mul.73
  59.8 0.1 mul.74
  59.9 0.1 broadcast.10.clone.1
  60.0 0.1 constant_dynamic-update-slice_fusion.3
  60.1 1.5 %collective-permute-start.3 = (bf16[256,512]{1,0:T(8,128)(2,1)S(1)}, bf16[256,512]{1,0:T(8,128)(2,1)S(1)}, u32[]{:S(2)}, u32[]{:S(2)}) collective-permute-start(bf16[256,512]{1,0:T(8,128)(2,1)S(1)} %get-tuple-element.6), channel_id=1, source_target_pairs={{0,8},{8,16},{16,24},{24,0},{1,9},{9,17},{17,25},{25,1},{2,10},{10... | collective-permute-start | bytes 786440 | tf_op jit(solution)/shard_map/ppermute | solution.py:16
  61.6 2.3 %collective-permute-start.4 = (bf16[256,512]{1,0:T(8,128)(2,1)S(1)}, bf16[256,512]{1,0:T(8,128)(2,1)S(1)}, u32[]{:S(2)}, u32[]{:S(2)}) collective-permute-start(bf16[256,512]{1,0:T(8,128)(2,1)S(1)} %get-tuple-element.6), channel_id=1, source_target_pairs={{0,24},{8,0},{16,8},{24,16},{1,25},{9,1},{17,9},{25,17},{2,26},{10... | collective-permute-start | bytes 786440 | tf_op jit(solution)/shard_map/ppermute | solution.py:21
  64.0 7.2 %collective-permute-done.3 = bf16[256,512]{1,0:T(8,128)(2,1)S(1)} collective-permute-done((bf16[256,512]{1,0:T(8,128)(2,1)S(1)}, bf16[256,512]{1,0:T(8,128)(2,1)S(1)}, u32[]{:S(2)}, u32[]{:S(2)}) %collective-permute-start.3) | collective-permute-done | bytes 262176 | tf_op jit(solution)/shard_map/ppermute | solution.py:16
  71.2 0.0 collective-permute-start.5
  71.2 4.3 %collective-permute-done.4 = bf16[256,512]{1,0:T(8,128)(2,1)S(1)} collective-permute-done((bf16[256,512]{1,0:T(8,128)(2,1)S(1)}, bf16[256,512]{1,0:T(8,128)(2,1)S(1)}, u32[]{:S(2)}, u32[]{:S(2)}) %collective-permute-start.4) | collective-permute-done | bytes 262176 | tf_op jit(solution)/shard_map/ppermute | solution.py:21
  75.5 5.8 %collective-permute-done.5 = bf16[256,512]{1,0:T(8,128)(2,1)S(1)} collective-permute-done((bf16[256,512]{1,0:T(8,128)(2,1)S(1)}, bf16[256,512]{1,0:T(8,128)(2,1)S(1)}, u32[]{:S(2)}, u32[]{:S(2)}) %collective-permute-start.5) | collective-permute-done | bytes 262176 | tf_op jit(solution)/shard_map/ppermute | solution.py:16
  81.3 0.0 all-gather.5.cloned.1.call-done
  81.3 2.0 %fusion.1 = f32[512,512]{0,1:T(8,128)S(1)} fusion(bf16[512,1024]{0,1:T(8,128)(2,1)} %all-gather.5.cloned.1.call-done, bf16[1024,512]{1,0:T(8,128)(2,1)S(1)} %constant_dynamic-update-slice_fusion), kind=kOutput, calls=%fused_computation.15 | convolution fusion | flops 536870912 | bytes 3145728 | tf_op jit(solution)/shard_map/dot_general | solution.py:55
  83.3 1.3 %copy.9 = f32[512,2,256]{2,0,1:T(8,128)} copy(f32[512,2,256]{0,2,1:T(8,128)S(1)} %bitcast.36) | data formatting | bytes 2097152 | tf_op jit(solution)/shard_map/reshape | solution.py:59
  84.6 0.0 reduce-scatter.5.cloned.1.call-update
  84.7 18.6 %reduce-scatter.5.cloned.1.call-done = f32[512,1,256]{2,0,1:T(8,128)} async-done(((f32[512,2,256]{2,0,1:T(8,128)}), f32[512,1,256]{2,0,1:T(8,128)}) %reduce-scatter.5.cloned.1.call-update) | async-done | bytes 524304 | tf_op jit(solution)/shard_map/reduce_scatter | solution.py:58
  103.3 1.8 %convert_element_type.59 = bf16[512,1,256]{2,0,1:T(8,128)(2,1)} convert(f32[512,1,256]{2,0,1:T(8,128)} %reduce-scatter.5.cloned.1.call-done) | non-fusion elementwise | flops 131072 | bytes 786432 | tf_op jit(solution)/shard_map/convert_element_type | solution.py:80
  (17 shorter events, 0.2 us)
Async XLA Ops:
  6.5 1.1 copy-start
  6.5 26.7 %all-gather.3.cloned.1.call-start = ((), (), s32[]{:S(2)}) async-start(), calls=%async_computation.2 | async-start | bytes 1310720 | tf_op jit(solution)/shard_map/all_gather | solution.py:51
  8.3 0.9 copy-start.1
  8.4 47.6 %reduce-scatter.3.cloned.1.call-start = ((), (), s32[]{:S(2)}) async-start(), calls=%async_computation.3 | async-start | bytes 1572864 | tf_op jit(solution)/shard_map/reduce_scatter | solution.py:58
  9.3 0.7 copy-start.3
  10.5 12.3 %collective-permute-start = (bf16[256,512]{1,0:T(8,128)(2,1)S(1)}, bf16[256,512]{1,0:T(8,128)(2,1)S(1)}, u32[]{:S(2)}, u32[]{:S(2)}) collective-permute-start(bf16[256,512]{1,0:T(8,128)(2,1)S(1)} %get-tuple-element.8), channel_id=1, source_target_pairs={{0,8},{8,16},{16,24},{24,0},{1,9},{9,17},{17,25},{25,1},{2,10},{10... | collective-permute-start | bytes 786440 | tf_op jit(solution)/shard_map/ppermute | solution.py:16
  13.5 13.6 %collective-permute-start.1 = (bf16[256,512]{1,0:T(8,128)(2,1)S(1)}, bf16[256,512]{1,0:T(8,128)(2,1)S(1)}, u32[]{:S(2)}, u32[]{:S(2)}) collective-permute-start(bf16[256,512]{1,0:T(8,128)(2,1)S(1)} %get-tuple-element.8), channel_id=1, source_target_pairs={{0,24},{8,0},{16,8},{24,16},{1,25},{9,1},{17,9},{25,17},{2,26},{10... | collective-permute-start | bytes 786440 | tf_op jit(solution)/shard_map/ppermute | solution.py:21
  22.7 10.4 %collective-permute-start.2 = (bf16[256,512]{1,0:T(8,128)(2,1)S(1)}, bf16[256,512]{1,0:T(8,128)(2,1)S(1)}, u32[]{:S(2)}, u32[]{:S(2)}) collective-permute-start(bf16[256,512]{1,0:T(8,128)(2,1)S(1)} %collective-permute-done), channel_id=1, source_target_pairs={{0,8},{8,16},{16,24},{24,0},{1,9},{9,17},{17,25},{25,1},{2,10},{10... | collective-permute-start | bytes 786440 | tf_op jit(solution)/shard_map/ppermute | solution.py:16
  36.2 0.7 copy-start.5
  36.2 45.1 %all-gather.5.cloned.1.call-start = ((), (), s32[]{:S(2)}) async-start(), calls=%async_computation.4 | async-start | bytes 1310720 | tf_op jit(solution)/shard_map/all_gather | solution.py:51
  58.0 0.9 copy-start.2
  58.0 45.3 %reduce-scatter.5.cloned.1.call-start = ((), (), s32[]{:S(2)}) async-start(), calls=%async_computation.5 | async-start | bytes 1572864 | tf_op jit(solution)/shard_map/reduce_scatter | solution.py:58
  58.9 0.7 copy-start.4
  60.1 11.1 %collective-permute-start.3 = (bf16[256,512]{1,0:T(8,128)(2,1)S(1)}, bf16[256,512]{1,0:T(8,128)(2,1)S(1)}, u32[]{:S(2)}, u32[]{:S(2)}) collective-permute-start(bf16[256,512]{1,0:T(8,128)(2,1)S(1)} %get-tuple-element.6), channel_id=1, source_target_pairs={{0,8},{8,16},{16,24},{24,0},{1,9},{9,17},{17,25},{25,1},{2,10},{10... | collective-permute-start | bytes 786440 | tf_op jit(solution)/shard_map/ppermute | solution.py:16
  61.6 13.9 %collective-permute-start.4 = (bf16[256,512]{1,0:T(8,128)(2,1)S(1)}, bf16[256,512]{1,0:T(8,128)(2,1)S(1)}, u32[]{:S(2)}, u32[]{:S(2)}) collective-permute-start(bf16[256,512]{1,0:T(8,128)(2,1)S(1)} %get-tuple-element.6), channel_id=1, source_target_pairs={{0,24},{8,0},{16,8},{24,16},{1,25},{9,1},{17,9},{25,17},{2,26},{10... | collective-permute-start | bytes 786440 | tf_op jit(solution)/shard_map/ppermute | solution.py:21
  71.2 10.1 %collective-permute-start.5 = (bf16[256,512]{1,0:T(8,128)(2,1)S(1)}, bf16[256,512]{1,0:T(8,128)(2,1)S(1)}, u32[]{:S(2)}, u32[]{:S(2)}) collective-permute-start(bf16[256,512]{1,0:T(8,128)(2,1)S(1)} %collective-permute-done.3), channel_id=1, source_target_pairs={{0,8},{8,16},{16,24},{24,0},{1,9},{9,17},{17,25},{25,1},{2,10},{10... | collective-permute-start | bytes 786440 | tf_op jit(solution)/shard_map/ppermute | solution.py:16
Sparse Core Ops, SparseCore 0:
  8.9 19.5 all-gather.2
  36.3 19.6 reduce-scatter.2
  58.1 16.7 all-gather.4
  84.8 18.4 reduce-scatter.4
